TPU v7x, 32 devices: a whole 2x2x4 slice. The times are simulated.
32 devices in a mesh: ep: 8 (over z, y), tp: 4 (over x, core).
Axes of the slice: x: 2, y: 2, z: 4, core: 2. Of those that a mesh axis runs over, the one named last changes fastest.
Arguments:
- tokens: bfloat16 [1024, 3584], P('ep', 'tp'), may hold values from -6 to 6
- tangents: bfloat16 [2, 1024, 3584], P(None, 'ep', 'tp'), may hold values from -6 to 6
- tangent_mask: int32 [2, 1024, 28], P(None, 'ep', 'tp'), may hold values 0 or 1
- expert_ids: int32 [1024, 2], P('ep'), may hold values from 0 to 7, all different within a row; in each aligned block of 128 rows (0 to 127, 128 to 255, ...) at most 48 rows name the same one
- gate_fixed: int32 [1024, 2], P('ep'), may hold values from 4096 to 65535
- w_up: bfloat16 [8, 3584, 1024], P('ep', None, 'tp'), may hold values from -0.09375 to 0.09375
- w_down: bfloat16 [8, 1024, 3584], P('ep', None, 'tp'), may hold values from -0.1875 to 0.1875
Outputs:
- mixed: bfloat16 [1024, 3584], P('ep', 'tp')
- mixed_tangents: bfloat16 [2, 1024, 3584], P(None, 'ep', 'tp')
Inputs may be any that keep to these rules, and one draw needn't show every extreme that they name: `expert_ids`: each row names 2 different experts; among the rows of the tokens of one index of ep (128 aligned rows) no expert is named by more than 48 rows, a bound that some block reaches.
All inputs are finite; a program needn't handle non-finite values. No bound on the sum of `tangent_mask` on one device may be relied on, other than what follows from the above.
Results may differ from a plain program's by a relative error of at most 0.008.
Values may be sent and summed in bfloat16 or wider, within the bound.
A program may use at most 64 MiB of HBM per device.

v0:
```python
import jax
import jax.numpy as jnp
from jax import lax
from jax.sharding import PartitionSpec as P


def body(tokens, tangents, tangent_mask, expert_ids, gate_fixed, w_up, w_down):
    group, quarter = tokens.shape
    n_ep = lax.axis_size("ep")
    top = expert_ids.shape[1]
    local_experts = w_up.shape[0]
    experts = local_experts * n_ep
    capacity = max(2, min(group, 3 * group * top // (2 * experts)))
    blocks = tangent_mask.shape[2]
    keep = tangent_mask.astype(jnp.bfloat16)
    masked = (tangents.reshape(2, group, blocks, quarter // blocks) * keep[..., None]).reshape(
        2, group, quarter
    )
    stacked = jnp.concatenate([tokens[None], masked], axis=0)
    flat_ids = expert_ids.reshape(-1)
    onehot = (flat_ids[:, None] == jnp.arange(experts, dtype=jnp.int32)[None, :]).astype(jnp.int32)
    rank = jnp.sum((jnp.cumsum(onehot, axis=0) - onehot) * onehot, axis=1)
    dest = flat_ids * capacity + rank
    owner = jnp.full((experts * capacity,), group, jnp.int32)
    owner = owner.at[dest].set(jnp.arange(group * top, dtype=jnp.int32) // top)
    send_cols = jnp.take(stacked, owner, axis=1, mode="fill", fill_value=0)
    send_cols = send_cols.reshape(3, n_ep, local_experts * capacity, quarter)
    arrived = lax.all_to_all(send_cols, "ep", split_axis=1, concat_axis=1, tiled=True)
    routed = arrived.reshape(3, n_ep, local_experts, capacity, quarter)
    weights = w_up
    hidden = jnp.einsum(
        "tsecd,edf->tsecf",
        lax.all_gather(routed, "tp", axis=4, tiled=True),
        weights,
        preferred_element_type=jnp.float32,
    )
    base = hidden[0]
    sig = jax.nn.sigmoid(base)
    slope = sig * (1.0 + base * (1.0 - sig))
    acts = jnp.concatenate([(base * sig)[None], slope[None] * hidden[1:]], axis=0).astype(
        jnp.bfloat16
    )
    out_width = w_down.shape[2]
    weights = w_down
    outs = jnp.einsum(
        "tsecf,efd->tsecd",
        lax.all_gather(acts, "tp", axis=4, tiled=True),
        weights,
        preferred_element_type=jnp.float32,
    ).astype(jnp.bfloat16)
    outs = outs.reshape(3, n_ep, local_experts * capacity, out_width)
    returned = lax.all_to_all(outs, "ep", split_axis=1, concat_axis=1, tiled=True)
    table = returned.reshape(3, experts * capacity, out_width)
    picked = jnp.take(table, dest, axis=1).reshape(3, group, top, out_width)
    gates = gate_fixed.astype(jnp.float32) / 65536.0
    summed = jnp.einsum("tgkd,gk->tgd", picked.astype(jnp.float32), gates).astype(jnp.bfloat16)
    return (summed[0], summed[1:])


def solution(mesh):
    placed = (
        P("ep", "tp"),
        P(None, "ep", "tp"),
        P(None, "ep", "tp"),
        P("ep", None),
        P("ep", None),
        P("ep", None, "tp"),
        P("ep", None, "tp"),
    )
    return jax.shard_map(
        body,
        mesh=mesh,
        in_specs=placed,
        out_specs=(P("ep", "tp"), P(None, "ep", "tp")),
        check_vma=False,
    )
```

profile of v0, /device:TPU:0, one launch (start us, length us, event | category | flops | bytes accessed | tf_op | source)
XLA Modules:
  0.0 249.6 jit_solution(13066110364712202970)
XLA Ops:
  7.2 0.0 copy-start
  7.2 0.0 all-gather.6.cloned.1.call-start
  7.2 1.0 copy.39
  8.2 0.1 eq.26
  8.3 0.1 reshape.144
  8.5 0.7 broadcast_multiply_fusion
  9.2 0.6 reduce-window.6
  9.8 0.2 slice_reduce_fusion
  10.0 0.1 copy.43
  10.1 0.1 mul.64
  10.3 0.1 fusion.16
  10.4 1.4 scatter_custom_fusion
  11.8 0.7 convert_element_type.38
  12.5 0.1 mul.65
  12.6 0.7 copy.46
  13.3 0.4 copy.47
  13.7 0.1 broadcast_in_dim.37
  13.8 1.6 copy_multiply_fusion
  15.4 0.9 pad_maximum_fusion
  16.4 5.0 %gather_fusion = bf16[384,3,896]{2,1,0:T(4,128)(2,1)} fusion(bf16[3,128,896]{2,0,1:T(4,128)(2,1)S(1)} %pad_maximum_fusion, s32[1024]{0:T(1024)S(1)} %pad_clamp_fusion.1), kind=kCustom, calls=%fused_computation | custom fusion | bytes 4130304 | tf_op jit(solution)/shard_map/jit(_take)/gather | solution.py:26
  21.4 2.2 copy_select_fusion
  23.6 54.6 %all_to_all.10 = bf16[3,8,48,896]{3,2,0,1:T(8,128)(2,1)S(1)} all-to-all(bf16[3,8,48,896]{3,2,0,1:T(8,128)(2,1)S(1)} %copy_select_fusion), channel_id=1, replica_groups=mesh['ep'=8,'tp'=4] {'ep'}, dimensions={1} | all-to-all | bytes 4128768 | tf_op jit(solution)/shard_map/all_to_all | solution.py:28
  78.2 1.6 copy.49
  79.8 0.0 all-gather.6.cloned.1.call-update
  79.8 0.0 all-gather.4.cloned.1.call-start
  79.9 56.6 %all-gather.6.cloned.1.call-done = bf16[3,8,48,3584]{3,2,1,0:T(8,128)(2,1)} async-done(((bf16[3,8,48,896]{3,2,1,0:T(8,128)(2,1)}), bf16[3,8,48,3584]{3,2,1,0:T(8,128)(2,1)}) %all-gather.6.cloned.1.call-update) | async-done | bytes 8257552 | tf_op jit(solution)/shard_map/all_gather | solution.py:33
  136.5 6.2 %fusion.8 = f32[3,8,1,48,256]{4,3,1,0,2:T(8,128)S(1)} fusion(bf16[3,8,48,3584]{3,2,1,0:T(8,128)(2,1)} %all-gather.6.cloned.1.call-done, bf16[1,3584,256]{2,1,0:T(8,128)(2,1)} %param.12), kind=kOutput, calls=%fused_computation.11 | convolution fusion | flops 2113929216 | bytes 11272192 | tf_op jit(solution)/shard_map/tsecd,edf->tsecf/dot_general | solution.py:31
  142.6 0.2 multiply_convert_fusion
  142.8 0.1 fusion.13
  142.9 0.9 pad_maximum_fusion.1
  143.8 0.0 all-gather.4.cloned.1.call-update
  143.8 24.5 %all-gather.4.cloned.1.call-done = bf16[3,8,1,48,1024]{4,3,1,0,2:T(8,128)(2,1)} async-done(((bf16[3,8,1,48,256]{4,3,1,0,2:T(8,128)(2,1)}), bf16[3,8,1,48,1024]{4,3,1,0,2:T(8,128)(2,1)}) %all-gather.4.cloned.1.call-update) | async-done | bytes 2359312 | tf_op jit(solution)/shard_map/all_gather | solution.py:47
  168.3 4.3 %fusion.2 = bf16[3,8,48,896]{3,2,1,0:T(8,128)(2,1)S(1)} fusion(bf16[3,8,1,48,1024]{4,3,1,0,2:T(8,128)(2,1)} %all-gather.4.cloned.1.call-done, bf16[1,1024,896]{2,1,0:T(8,128)(2,1)S(1)} %copy-done), kind=kOutput, calls=%fused_computation.6 | convolution fusion | flops 2114961408 | bytes 6258688 | tf_op jit(solution)/shard_map/tsecf,efd->tsecd/dot_general | solution.py:45
  172.6 1.5 copy.50
  174.1 5.6 %all-to-all-start.1 = ((bf16[3,8,48,896]{3,2,0,1:T(8,128)(2,1)}), bf16[3,8,48,896]{3,2,0,1:T(8,128)(2,1)}, u32[]{:S(2)}, u32[]{:S(2)}) async-start(bf16[3,8,48,896]{3,2,0,1:T(8,128)(2,1)} %copy.50), calls=%async_computation.1 | async-start | bytes 4128768 | tf_op jit(solution)/shard_map/all_to_all | solution.py:52
  179.7 0.1 reduce_sum.14
  179.9 0.1 copy.41
  180.0 0.1 copy.42
  180.1 0.0 copy-done.3
  180.1 0.1 copy.54
  180.3 47.5 %all-to-all-done.1 = bf16[3,8,48,896]{3,2,0,1:T(8,128)(2,1)} async-done(((bf16[3,8,48,896]{3,2,0,1:T(8,128)(2,1)}), bf16[3,8,48,896]{3,2,0,1:T(8,128)(2,1)}, u32[]{:S(2)}, u32[]{:S(2)}) %all-to-all-start.1) | async-done | bytes 2064416 | tf_op jit(solution)/shard_map/all_to_all | solution.py:52
  227.8 4.3 %copy.51 = bf16[3,8,48,896]{3,0,2,1:T(4,128)(2,1)} copy(bf16[3,8,48,896]{3,2,0,1:T(8,128)(2,1)} %all-to-all-done.1) | data formatting | bytes 4128768 | tf_op jit(solution)/shard_map/all_to_all | solution.py:52
  232.1 5.2 %gather_fusion.1 = bf16[256,3,896]{2,1,0:T(4,128)(2,1)} fusion(bf16[3,384,896]{2,0,1:T(4,128)(2,1)} %bitcast.63, s32[1024]{0:T(1024)S(1)} %pad_clamp_fusion), kind=kCustom, calls=%fused_computation.1 | custom fusion | bytes 2753536 | tf_op jit(solution)/shard_map/jit(_take)/gather | solution.py:54
  237.2 2.3 broadcast_select_fusion
  239.5 1.6 fusion.11
  241.2 0.1 copy.64
  241.2 0.8 slice.32
  242.1 0.7 slice_bitcast_fusion
  (18 shorter events, 0.1 us)
Async XLA Ops:
  7.2 161.1 %copy-start = (bf16[1,1024,896]{2,1,0:T(8,128)(2,1)S(1)}, bf16[1,1024,896]{2,1,0:T(8,128)(2,1)}, u32[]{:S(2)}) copy-start(bf16[1,1024,896]{2,1,0:T(8,128)(2,1)} %param.13) | copy-start | bytes 5505028
  7.2 6.2 %copy-start.1 = (bf16[128,896]{1,0:T(8,128)(2,1)S(1)}, bf16[128,896]{1,0:T(8,128)(2,1)}, u32[]{:S(2)}) copy-start(bf16[128,896]{1,0:T(8,128)(2,1)} %param.7) | copy-start | bytes 688132
  7.2 129.3 %all-gather.6.cloned.1.call-start = ((), (), s32[]{:S(2)}) async-start(), calls=%async_computation.3 | async-start | bytes 10321920 | tf_op jit(solution)/shard_map/all_gather | solution.py:33
  79.8 88.5 %all-gather.4.cloned.1.call-start = ((), (), s32[]{:S(2)}) async-start(), calls=%async_computation.2 | async-start | bytes 2949120 | tf_op jit(solution)/shard_map/all_gather | solution.py:47
  174.1 5.9 %copy-start.2 = (s32[128,2]{0,1:T(2,128)S(1)}, s32[128,2]{0,1:T(2,128)}, u32[]{:S(2)}) copy-start(s32[128,2]{0,1:T(2,128)} %param.10) | copy-start | bytes 3076
  174.1 6.0 %copy-start.3 = (s32[128,2]{0,1:T(2,128)S(1)}, s32[128,2]{0,1:T(2,128)}, u32[]{:S(2)}) copy-start(s32[128,2]{0,1:T(2,128)} %param.11) | copy-start | bytes 3076
  174.1 53.7 %all-to-all-start.1 = ((bf16[3,8,48,896]{3,2,0,1:T(8,128)(2,1)}), bf16[3,8,48,896]{3,2,0,1:T(8,128)(2,1)}, u32[]{:S(2)}, u32[]{:S(2)}) async-start(bf16[3,8,48,896]{3,2,0,1:T(8,128)(2,1)} %copy.50), calls=%async_computation.1 | async-start | bytes 4128768 | tf_op jit(solution)/shard_map/all_to_all | solution.py:52
Sparse Core Ops, SparseCore 0:
  79.9 56.4 all-gather.5
  143.9 24.3 all-gather.3
where the time goes:
time: 250 us
  waiting for transfers between devices  129 us (52%)
  blocking collectives  54.6 us (22%)
  local copies, waits for them, and re-layouts  24 us (10%)
  between operations  14.2 us (6%)
  matrix products  12.1 us (5%)
  other arithmetic  10.3 us (4%)
  starting transfers between devices  5.73 us (2%)
    all_gather x1, waiting for transfers between devices, body(): lax.all_gather(routed, 'tp', axis=4, tiled=True)  56.6 us
    all_to_all x1, blocking collectives, body(): lax.all_to_all(send_cols, 'ep', split_axis=1, concat_axis=1, tiled=True)  54.6 us
    all_to_all x1, waiting for transfers between devices, body(): lax.all_to_all(outs, 'ep', split_axis=1, concat_axis=1, tiled=True)  47.5 us
    all_gather x1, waiting for transfers between devices, body(): lax.all_gather(acts, 'tp', axis=4, tiled=True)  24.5 us
    dot_general x1, matrix products, body(): jnp.einsum('tsecd,edf->tsecf', lax.all_gather(routed, 'tp', axis=4, tiled...  6.16 us
    all_to_all x1, starting transfers between devices, body(): lax.all_to_all(outs, 'ep', split_axis=1, concat_axis=1, tiled=True)  5.65 us
    gather x1, local copies, waits for them, and re-layouts, body(): picked = jnp.take(table, dest, axis=1).reshape(3, group, top, out_width)  5.17 us
    gather x1, local copies, waits for them, and re-layouts, body(): send_cols = jnp.take(stacked, owner, axis=1, mode='fill', fill_value=0)  5.02 us
  transfers between devices with their start and end apart: 3, of which 3 were waited for; matrix products, arithmetic and copies ran while one was open for 0% of the time, Pallas kernels for 0%

commit v1 on v0

--- a/solution.py
+++ b/solution.py
@@ -2,6 +2,17 @@
 import jax.numpy as jnp
 from jax import lax
 from jax.sharding import PartitionSpec as P
+
+
+def ring_gather(shard, axis, dim):
+    ways = lax.axis_size(axis)
+    pieces = [shard]
+    for far in range(1, ways):
+        pieces.append(
+            lax.ppermute(pieces[far - 1], axis, [(d, (d - 1) % ways) for d in range(ways)])
+        )
+    line = jnp.concatenate(pieces, axis=dim)
+    return jnp.roll(line, lax.axis_index(axis) * shard.shape[dim], axis=dim)
 
 
 def body(tokens, tangents, tangent_mask, expert_ids, gate_fixed, w_up, w_down):
@@ -43,10 +54,7 @@
     out_width = w_down.shape[2]
     weights = w_down
     outs = jnp.einsum(
-        "tsecf,efd->tsecd",
-        lax.all_gather(acts, "tp", axis=4, tiled=True),
-        weights,
-        preferred_element_type=jnp.float32,
+        "tsecf,efd->tsecd", ring_gather(acts, "tp", 4), weights, preferred_element_type=jnp.float32
     ).astype(jnp.bfloat16)
     outs = outs.reshape(3, n_ep, local_experts * capacity, out_width)
     returned = lax.all_to_all(outs, "ep", split_axis=1, concat_axis=1, tiled=True)

time: 250 us -> 261 us (1.044)
  local copies, waits for them, and re-layouts: 24 us -> 32.4 us
  starting transfers between devices: 5.73 us -> 9.91 us
  waiting for transfers between devices: 129 us -> 125 us
    all_gather x1 -> x0, waiting for transfers between devices: 24.5 us -> none  [body(): lax.all_gather(acts, 'tp', axis=4, tiled=True)]
    ppermute x0 -> x3, waiting for transfers between devices: none -> 20.4 us  [ring_gather(): lax.ppermute(pieces[far - 1], axis, [(d, (d - 1) % ways) for d in range(w...]
    unnamed x9 -> x16, local copies, waits for them, and re-layouts: 0.99 us -> 6.5 us
    ppermute x0 -> x3, starting transfers between devices: none -> 4.02 us  [ring_gather(): lax.ppermute(pieces[far - 1], axis, [(d, (d - 1) % ways) for d in range(w...]
  transfers between devices with their start and end apart: 3 -> 5, of which waited for: 3 -> 5; matrix products, arithmetic and copies ran while one was open for 0% -> 1% of each run, Pallas kernels for 0% -> 0%
where the time goes in v1:
time: 261 us; the launch traced here: 260 us
  waiting for transfers between devices  125 us (48%)
  blocking collectives  54.6 us (21%)
  local copies, waits for them, and re-layouts  32.4 us (12%)
  between operations  14.2 us (5%)
  matrix products  12.1 us (5%)
  other arithmetic  11.4 us (4%)
  starting transfers between devices  9.91 us (4%)
    all_gather x1, waiting for transfers between devices, body(): lax.all_gather(routed, 'tp', axis=4, tiled=True)  56.6 us
    all_to_all x1, blocking collectives, body(): lax.all_to_all(send_cols, 'ep', split_axis=1, concat_axis=1, tiled=True)  54.6 us
    all_to_all x1, waiting for transfers between devices, body(): lax.all_to_all(outs, 'ep', split_axis=1, concat_axis=1, tiled=True)  48.3 us
    ppermute x3, waiting for transfers between devices, ring_gather(): lax.ppermute(pieces[far - 1], axis, [(d, (d - 1) % ways) for d in range(w...  20.4 us
    unnamed x16, local copies, waits for them, and re-layouts  6.5 us
    dot_general x1, matrix products, body(): jnp.einsum('tsecd,edf->tsecf', lax.all_gather(routed, 'tp', axis=4, tiled...  6.16 us
    all_to_all x1, starting transfers between devices, body(): lax.all_to_all(outs, 'ep', split_axis=1, concat_axis=1, tiled=True)  5.86 us
  transfers between devices with their start and end apart: 5, of which 5 were waited for; matrix products, arithmetic and copies ran while one was open for 1% of the time, Pallas kernels for 0%

profile of v1, /device:TPU:0, one launch (start us, length us, event | category | flops | bytes accessed | tf_op | source)
XLA Modules:
  0.0 259.9 jit_solution(14551567585996277777)
XLA Ops:
  7.2 0.9 copy.39
  8.1 0.1 eq.29
  8.3 0.1 reshape.144
  8.4 0.7 broadcast_multiply_fusion
  9.1 0.6 reduce-window.6
  9.7 0.2 slice_reduce_fusion
  10.1 0.1 mul.67
  10.3 1.4 scatter_custom_fusion
  11.8 0.7 convert_element_type.38
  12.5 0.7 copy.46
  13.3 1.3 copy.47
  14.7 1.6 copy_multiply_fusion
  16.3 0.9 pad_maximum_fusion
  17.2 5.0 %gather_fusion = bf16[384,3,896]{2,1,0:T(4,128)(2,1)} fusion(bf16[3,128,896]{2,0,1:T(4,128)(2,1)S(1)} %pad_maximum_fusion, s32[1024]{0:T(1024)S(1)} %pad_clamp_fusion.1), kind=kCustom, calls=%fused_computation | custom fusion | bytes 4130304 | tf_op jit(solution)/shard_map/jit(_take)/gather | solution.py:37
  22.3 2.2 copy_select_fusion
  24.5 54.6 %all_to_all.10 = bf16[3,8,48,896]{3,2,0,1:T(8,128)(2,1)S(1)} all-to-all(bf16[3,8,48,896]{3,2,0,1:T(8,128)(2,1)S(1)} %copy_select_fusion), channel_id=1, replica_groups=mesh['ep'=8,'tp'=4] {'ep'}, dimensions={1} | all-to-all | bytes 4128768 | tf_op jit(solution)/shard_map/all_to_all | solution.py:39
  79.1 1.6 copy.49
  80.7 56.6 %all-gather.3.cloned.1.call-done = bf16[3,8,48,3584]{3,2,1,0:T(8,128)(2,1)} async-done(((bf16[3,8,48,896]{3,2,1,0:T(8,128)(2,1)}), bf16[3,8,48,3584]{3,2,1,0:T(8,128)(2,1)}) %all-gather.3.cloned.1.call-update) | async-done | bytes 8257552 | tf_op jit(solution)/shard_map/all_gather | solution.py:44
  137.3 6.2 %fusion.9 = f32[3,8,1,48,256]{4,3,1,0,2:T(8,128)S(1)} fusion(bf16[3,8,48,3584]{3,2,1,0:T(8,128)(2,1)} %all-gather.3.cloned.1.call-done, bf16[1,3584,256]{2,1,0:T(8,128)(2,1)} %param.12), kind=kOutput, calls=%fused_computation.12 | convolution fusion | flops 2113929216 | bytes 11272192 | tf_op jit(solution)/shard_map/tsecd,edf->tsecf/dot_general | solution.py:42
  143.5 0.2 multiply_convert_fusion
  143.6 0.1 fusion.14
  143.8 1.0 pad_maximum_fusion.1
  144.8 0.2 collective-permute-start
  145.0 7.4 %collective-permute-done = bf16[3,8,1,48,256]{4,3,1,0,2:T(8,128)(2,1)S(1)} collective-permute-done((bf16[3,8,1,48,256]{4,3,1,0,2:T(8,128)(2,1)S(1)}, bf16[3,8,1,48,256]{4,3,1,0,2:T(8,128)(2,1)S(1)}, u32[]{:S(2)}, u32[]{:S(2)}) %collective-permute-start) | collective-permute-done | bytes 589856 | tf_op jit(solution)/shard_map/ppermute | solution.py:12
  152.4 1.9 collective-permute-start.1
  154.3 7.4 %collective-permute-done.1 = bf16[3,8,1,48,256]{4,3,1,0,2:T(8,128)(2,1)S(1)} collective-permute-done((bf16[3,8,1,48,256]{4,3,1,0,2:T(8,128)(2,1)S(1)}, bf16[3,8,1,48,256]{4,3,1,0,2:T(8,128)(2,1)S(1)}, u32[]{:S(2)}, u32[]{:S(2)}) %collective-permute-start.1) | collective-permute-done | bytes 589856 | tf_op jit(solution)/shard_map/ppermute | solution.py:12
  161.7 1.9 collective-permute-start.2
  163.6 0.9 constant_dynamic-update-slice_fusion.6
  164.5 0.9 constant_dynamic-update-slice_fusion.5
  165.4 5.6 %collective-permute-done.2 = bf16[3,8,1,48,256]{4,3,1,0,2:T(8,128)(2,1)} collective-permute-done((bf16[3,8,1,48,256]{4,3,1,0,2:T(8,128)(2,1)S(1)}, bf16[3,8,1,48,256]{4,3,1,0,2:T(8,128)(2,1)}, u32[]{:S(2)}, u32[]{:S(2)}) %collective-permute-start.2) | collective-permute-done | bytes 589856 | tf_op jit(solution)/shard_map/ppermute | solution.py:12
  171.0 2.0 constant_dynamic-update-slice_fusion.4
  173.0 0.9 constant_dynamic-update-slice_fusion.3
  173.8 0.9 constant_dynamic-update-slice_fusion.2
  174.7 0.9 constant_dynamic-update-slice_fusion.1
  175.6 2.0 constant_dynamic-update-slice_fusion
  177.6 4.3 %fusion.3 = bf16[3,8,48,896]{3,2,1,0:T(8,128)(2,1)S(1)} fusion(bf16[3,8,1,48,2048]{4,3,1,0,2:T(8,128)(2,1)} %constant_dynamic-update-slice_fusion, s32[]{:T(128)S(6)} %select_n.56, bf16[1,1024,896]{2,1,0:T(8,128)(2,1)S(1)} %copy-done), kind=kOutput, calls=%fused_computation.7 | convolution fusion | flops 2114961408 | bytes 6258692 | tf_op jit(solution)/shard_map/tsecf,efd->tsecd/dot_general | solution.py:56
  181.9 1.5 copy.50
  183.4 5.9 %all-to-all-start.1 = ((bf16[3,8,48,896]{3,2,0,1:T(8,128)(2,1)}), bf16[3,8,48,896]{3,2,0,1:T(8,128)(2,1)}, u32[]{:S(2)}, u32[]{:S(2)}) async-start(bf16[3,8,48,896]{3,2,0,1:T(8,128)(2,1)} %copy.50), calls=%async_computation.1 | async-start | bytes 4128768 | tf_op jit(solution)/shard_map/all_to_all | solution.py:60
  189.2 0.1 reduce_sum.14
  189.5 0.1 copy.42
  189.6 0.1 copy.54
  189.8 48.3 %all-to-all-done.1 = bf16[3,8,48,896]{3,2,0,1:T(8,128)(2,1)} async-done(((bf16[3,8,48,896]{3,2,0,1:T(8,128)(2,1)}), bf16[3,8,48,896]{3,2,0,1:T(8,128)(2,1)}, u32[]{:S(2)}, u32[]{:S(2)}) %all-to-all-start.1) | async-done | bytes 2064416 | tf_op jit(solution)/shard_map/all_to_all | solution.py:60
  238.1 4.3 %copy.51 = bf16[3,8,48,896]{3,0,2,1:T(4,128)(2,1)} copy(bf16[3,8,48,896]{3,2,0,1:T(8,128)(2,1)} %all-to-all-done.1) | data formatting | bytes 4128768 | tf_op jit(solution)/shard_map/all_to_all | solution.py:60
  242.4 5.2 %gather_fusion.1 = bf16[256,3,896]{2,1,0:T(4,128)(2,1)} fusion(bf16[3,384,896]{2,0,1:T(4,128)(2,1)} %bitcast.63, s32[1024]{0:T(1024)S(1)} %pad_clamp_fusion), kind=kCustom, calls=%fused_computation.1 | custom fusion | bytes 2753536 | tf_op jit(solution)/shard_map/jit(_take)/gather | solution.py:62
  247.6 2.3 broadcast_select_fusion
  249.8 1.6 fusion.12
  251.6 0.8 slice.32
  252.4 0.7 slice_bitcast_fusion
  (30 shorter events, 0.7 us)
Async XLA Ops:
  7.2 170.4 %copy-start = (bf16[1,1024,896]{2,1,0:T(8,128)(2,1)S(1)}, bf16[1,1024,896]{2,1,0:T(8,128)(2,1)}, u32[]{:S(2)}) copy-start(bf16[1,1024,896]{2,1,0:T(8,128)(2,1)} %param.13) | copy-start | bytes 5505028
  7.2 130.1 %all-gather.3.cloned.1.call-start = ((), (), s32[]{:S(2)}) async-start(), calls=%async_computation.2 | async-start | bytes 10321920 | tf_op jit(solution)/shard_map/all_gather | solution.py:44
  143.6 18.0 %copy-start.1 = (bf16[1,8,1,48,256]{4,3,1,0,2:T(8,128)(2,1)}, bf16[1,8,1,48,256]{4,3,1,0,2:T(8,128)(2,1)S(1)}, u32[]{:S(2)}) copy-start(bf16[1,8,1,48,256]{4,3,1,0,2:T(8,128)(2,1)S(1)} %get-tuple-element.2) | copy-start | bytes 589828
  144.8 7.6 %collective-permute-start = (bf16[3,8,1,48,256]{4,3,1,0,2:T(8,128)(2,1)S(1)}, bf16[3,8,1,48,256]{4,3,1,0,2:T(8,128)(2,1)S(1)}, u32[]{:S(2)}, u32[]{:S(2)}) collective-permute-start(bf16[3,8,1,48,256]{4,3,1,0,2:T(8,128)(2,1)S(1)} %get-tuple-element.4), channel_id=1, source_target_pairs={{0,3},{1,0},{2,1},{3,2},{4,7},{5,4},{6,5},{7,6},{8,11},{9,8},{10,9... | collective-permute-start | bytes 1769480 | tf_op jit(solution)/shard_map/ppermute | solution.py:12
  152.4 9.3 %collective-permute-start.1 = (bf16[3,8,1,48,256]{4,3,1,0,2:T(8,128)(2,1)S(1)}, bf16[3,8,1,48,256]{4,3,1,0,2:T(8,128)(2,1)S(1)}, u32[]{:S(2)}, u32[]{:S(2)}) collective-permute-start(bf16[3,8,1,48,256]{4,3,1,0,2:T(8,128)(2,1)S(1)} %collective-permute-done), channel_id=1, source_target_pairs={{0,3},{1,0},{2,1},{3,2},{4,7},{5,4},{6,5},{7,6},{8,11},{9,8},{10,9... | collective-permute-start | bytes 1769480 | tf_op jit(solution)/shard_map/ppermute | solution.py:12
  161.7 9.3 %collective-permute-start.2 = (bf16[3,8,1,48,256]{4,3,1,0,2:T(8,128)(2,1)S(1)}, bf16[3,8,1,48,256]{4,3,1,0,2:T(8,128)(2,1)}, u32[]{:S(2)}, u32[]{:S(2)}) collective-permute-start(bf16[3,8,1,48,256]{4,3,1,0,2:T(8,128)(2,1)S(1)} %collective-permute-done.1), channel_id=1, source_target_pairs={{0,3},{1,0},{2,1},{3,2},{4,7},{5,4},{6,5},{7,6},{8,11},{9,8},{10,9... | collective-permute-start | bytes 1769480 | tf_op jit(solution)/shard_map/ppermute | solution.py:12
  163.6 9.4 %copy-start.2 = (bf16[1,8,1,48,256]{4,3,1,0,2:T(8,128)(2,1)S(1)}, bf16[1,8,1,48,256]{4,3,1,0,2:T(8,128)(2,1)}, u32[]{:S(2)}) copy-start(bf16[1,8,1,48,256]{4,3,1,0,2:T(8,128)(2,1)} %copy-done.1) | copy-start | bytes 589828
  183.4 6.1 %copy-start.3 = (s32[128,2]{0,1:T(2,128)S(1)}, s32[128,2]{0,1:T(2,128)}, u32[]{:S(2)}) copy-start(s32[128,2]{0,1:T(2,128)} %param.10) | copy-start | bytes 3076
  183.4 6.2 %copy-start.4 = (s32[128,2]{0,1:T(2,128)S(1)}, s32[128,2]{0,1:T(2,128)}, u32[]{:S(2)}) copy-start(s32[128,2]{0,1:T(2,128)} %param.11) | copy-start | bytes 3076
  183.4 54.7 %all-to-all-start.1 = ((bf16[3,8,48,896]{3,2,0,1:T(8,128)(2,1)}), bf16[3,8,48,896]{3,2,0,1:T(8,128)(2,1)}, u32[]{:S(2)}, u32[]{:S(2)}) async-start(bf16[3,8,48,896]{3,2,0,1:T(8,128)(2,1)} %copy.50), calls=%async_computation.1 | async-start | bytes 4128768 | tf_op jit(solution)/shard_map/all_to_all | solution.py:60
Sparse Core Ops, SparseCore 0:
  80.8 56.4 all-gather.2
